TPU v7x, 256 devices: a whole 4x4x8 slice. The times are simulated.
256 devices in a mesh: ty: 8 (over y, z_hi), tx: 16 (over x, z_lo), pa: 2 (over core).
Axes of the slice: x: 4, y: 4, z: 8 (z_hi: 2, z_lo: 4; z = z_hi * 4 + z_lo), core: 2. Of those that a mesh axis runs over, the one named last changes fastest.
Arguments:
- object_field: float32 [2, 8192, 4096], P(None, 'ty', 'tx'), may hold values from -6 to 6
- probe_field: float32 [2, 128, 128], replicated, may hold values from -6 to 6
- amplitudes: bfloat16 [8, 16, 128, 128, 128], P('ty', 'tx', 'pa'), may hold values from 0.049804688 to 1.5
- start_row: int32 [8, 16, 128], P('ty', 'tx', 'pa'), may hold values from 0 to 1023
- start_col: int32 [8, 16, 128], P('ty', 'tx', 'pa'), may hold values from 0 to 255
- counts: int32 [8, 16], replicated, may hold values from 16 to 96, as said below
Outputs:
- object_grad: float32 [2, 8192, 4096], P(None, 'ty', 'tx')
- probe_grad: float32 [2, 128, 128], replicated
Inputs may be any that keep to these rules, and one draw needn't show every extreme that they name: Tile (a, b) uses its first counts[a, b] slots; some tile uses exactly 96.
All inputs are finite; a program needn't handle non-finite values.
Results may differ from a plain program's by a relative error of at most 0.0007.
The roundings to bfloat16 on the way count: a program that leaves them out, or rounds other values in their place, can miss the bound.
Values may be sent and summed in bfloat16 or wider, within the bound.
A program may use at most 64 MiB of HBM per device.

v0:
```python
import math
import jax
import jax.numpy as jnp
from jax import lax
from jax.sharding import PartitionSpec as P

BLK = 8


def from_behind(value, axis, steps):
    count = lax.axis_size(axis)
    initial, last = (max(0, -steps), min(count, count - steps))
    return lax.ppermute(value, axis, [(source, source + steps) for source in range(initial, last)])


def dft_table(length, inverse):
    freqs = jnp.arange(length, dtype=jnp.int32)
    phase = freqs[:, None] * freqs[None, :] % length
    angle = phase.astype(jnp.float32) * (2.0 * math.pi / length)
    scale = 1.0 / math.sqrt(length)
    cosine = jnp.cos(angle) * scale
    sine = jnp.sin(angle) * scale
    if inverse:
        upper = jnp.concatenate([cosine, sine], axis=1)
        lower = jnp.concatenate([-sine, cosine], axis=1)
    else:
        upper = jnp.concatenate([cosine, -sine], axis=1)
        lower = jnp.concatenate([sine, cosine], axis=1)
    return jnp.concatenate([upper, lower], axis=0).astype(jnp.bfloat16)


def along_last(real_part, imag_part, table):
    length = real_part.shape[-1]
    stacked = jnp.concatenate([real_part, imag_part], axis=-1)
    result = jnp.einsum("bnk,kj->bnj", stacked, table, preferred_element_type=jnp.float32)
    return (result[..., :length], result[..., length:])


def patch_terms(patches, measured, probe_field, usable, forward_table, inverse_table):
    probe_re = probe_field[0]
    probe_im = probe_field[1]
    patch_re = patches[:, 0]
    patch_im = patches[:, 1]
    psi_re = (probe_re * patch_re - probe_im * patch_im).astype(jnp.bfloat16)
    psi_im = (probe_re * patch_im + probe_im * patch_re).astype(jnp.bfloat16)
    half_re, half_im = along_last(psi_re, psi_im, forward_table)
    half_re = jnp.swapaxes(half_re.astype(jnp.bfloat16), 1, 2)
    half_im = jnp.swapaxes(half_im.astype(jnp.bfloat16), 1, 2)
    wave_re, wave_im = along_last(half_re, half_im, forward_table)
    level = jnp.swapaxes(measured, 1, 2).astype(jnp.float32)
    modulus = jnp.sqrt(wave_re * wave_re + wave_im * wave_im + 1.0)
    factor = jnp.where(usable[:, None, None], 1.0 - level / modulus, 0.0)
    chi_re = (wave_re * factor).astype(jnp.bfloat16)
    chi_im = (wave_im * factor).astype(jnp.bfloat16)
    back_re, back_im = along_last(chi_re, chi_im, inverse_table)
    back_re = jnp.swapaxes(back_re.astype(jnp.bfloat16), 1, 2)
    back_im = jnp.swapaxes(back_im.astype(jnp.bfloat16), 1, 2)
    grad_re, grad_im = along_last(back_re, back_im, inverse_table)
    object_re = probe_re * grad_re + probe_im * grad_im
    object_im = probe_re * grad_im - probe_im * grad_re
    probe_part_re = jnp.sum(patch_re * grad_re + patch_im * grad_im, axis=0)
    probe_part_im = jnp.sum(patch_re * grad_im - patch_im * grad_re, axis=0)
    return (object_re, object_im, jnp.stack([probe_part_re, probe_part_im]))


def shards(object_field, probe_field, amplitudes, start_row, start_col, counts):
    width = probe_field.shape[-1]
    tile_height = object_field.shape[1]
    tile_width = object_field.shape[2]
    half = start_row.shape[-1]
    row_place = lax.axis_index("ty")
    col_place = lax.axis_index("tx")
    core_place = lax.axis_index("pa")
    count = counts[row_place, col_place]
    zero = jnp.int32(0)
    right = from_behind(object_field[:, :, :width], "tx", -1)
    wider = jnp.concatenate([object_field, right], axis=2)
    below = from_behind(wider[:, :width, :], "ty", -1)
    extended = jnp.concatenate([wider, below], axis=1)
    rows_list = start_row[0, 0]
    cols_list = start_col[0, 0]
    measured_list = amplitudes[0, 0]
    nvalid = jnp.clip(count - core_place * half, 0, half)
    forward_table = dft_table(width, False)
    inverse_table = dft_table(width, True)

    def block_step(block_index, carry):
        grad_field, probe_acc = carry
        first = block_index * BLK
        block_rows = lax.dynamic_slice_in_dim(rows_list, first, BLK)
        block_cols = lax.dynamic_slice_in_dim(cols_list, first, BLK)
        measured = lax.dynamic_slice_in_dim(measured_list, first, BLK)
        usable = first + jnp.arange(BLK, dtype=jnp.int32) < nvalid
        patches = jnp.stack(
            [
                lax.dynamic_slice(
                    extended, (zero, block_rows[member], block_cols[member]), (2, width, width)
                )
                for member in range(BLK)
            ]
        )
        object_re, object_im, probe_part = patch_terms(
            patches, measured, probe_field, usable, forward_table, inverse_table
        )
        for member in range(BLK):
            where_at = (zero, block_rows[member], block_cols[member])
            current = lax.dynamic_slice(grad_field, where_at, (2, width, width))
            added = current + jnp.stack([object_re[member], object_im[member]])
            grad_field = lax.dynamic_update_slice(grad_field, added, where_at)
        return (grad_field, probe_acc + probe_part)

    nblocks = (nvalid + BLK - 1) // BLK
    init = (jnp.zeros(extended.shape, jnp.float32), jnp.zeros((2, width, width), jnp.float32))
    grad_field, probe_acc = lax.fori_loop(0, nblocks, block_step, init)
    right_strip = grad_field[:, :, tile_width:]
    arrived = from_behind(right_strip, "tx", 1)
    grad_field = grad_field[:, :, :tile_width].at[:, :, :width].add(arrived)
    lower_strip = grad_field[:, tile_height:, :]
    arrived_below = from_behind(lower_strip, "ty", 1)
    tile_grad = grad_field[:, :tile_height, :].at[:, :width, :].add(arrived_below)
    object_grad = lax.psum(tile_grad, "pa")
    probe_total = lax.psum(probe_acc, ("ty", "tx", "pa"))
    probe_grad = probe_total / jnp.sum(counts).astype(jnp.float32)
    return (object_grad, probe_grad)


def solution(mesh):
    return jax.shard_map(
        shards,
        mesh=mesh,
        in_specs=(
            P(None, "ty", "tx"),
            P(),
            P("ty", "tx", "pa", None, None),
            P("ty", "tx", "pa"),
            P("ty", "tx", "pa"),
            P(),
        ),
        out_specs=(P(None, "ty", "tx"), P()),
        check_vma=False,
    )
```

profile of v0, /device:TPU:1, one launch (start us, length us, event | category | flops | bytes accessed | tf_op | source)
XLA Modules:
  0.0 1034.8 jit_solution(16384427669747535714)
XLA Ops:
  10.1 23.9 %collective-permute-done = f32[2,1024,128]{2,1,0:T(8,128)S(1)} collective-permute-done((f32[2,1024,128]{2,1,0:T(8,128)S(1)}, f32[2,1024,128]{2,1,0:T(8,128)S(1)}, u32[]{:S(2)}, u32[]{:S(2)}) %collective-permute-start) | collective-permute-done | bytes 1048608 | tf_op jit(solution)/shard_map/ppermute | solution.py:13
  34.1 1.7 copy-done
  38.4 3.2 copy.10
  42.2 11.7 %collective-permute-done.1 = f32[2,128,384]{2,1,0:T(8,128)S(1)} collective-permute-done((f32[2,128,384]{2,1,0:T(8,128)S(1)}, f32[2,128,384]{2,1,0:T(8,128)S(1)}, u32[]{:S(2)}, u32[]{:S(2)}) %collective-permute-start.1) | collective-permute-done | bytes 393248 | tf_op jit(solution)/shard_map/ppermute | solution.py:13
  53.9 3.9 pad_maximum_fusion
  57.8 2.0 broadcast_in_dim.23
  59.8 81.8 %while.14 = (s32[]{:T(128)}, f32[2,1152,384]{2,1,0:T(8,128)}, f32[2,128,128]{2,1,0:T(8,128)S(1)}, s32[]{:T(128)}, s32[64]{0:T(128)S(1)}, /*index=5*/s32[64]{0:T(...) while((s32[]{:T(128)}, f32[2,1152,384]{2,1,0:T(8,128)}, ...), condition=%wide.region_3.4_spmd, body=%wide.region_0.3_spmd.sunk | while | flops 546603072 | bytes 25953520 | solution.py:114
  104.6 3.7 dynamic_update_slice.32
  109.3 3.7 dynamic_update_slice.33
  114.1 3.7 dynamic_update_slice.34
  118.9 3.7 dynamic_update_slice.35
  123.7 3.7 dynamic_update_slice.36
  128.5 3.7 dynamic_update_slice.37
  133.2 3.7 dynamic_update_slice.38
  137.9 3.7 dynamic_update_slice.39
  144.4 1.8 slice.222
  146.2 11.2 %collective-permute-done.2 = f32[2,1152,128]{2,1,0:T(8,128)S(1)} collective-permute-done((f32[2,1152,128]{2,1,0:T(8,128)S(1)}, f32[2,1152,128]{2,1,0:T(8,128)S(1)}, u32[]{:S(2)}, u32[]{:S(2)}) %collective-permute-start.2) | collective-permute-done | bytes 1179680 | tf_op jit(solution)/shard_map/ppermute | solution.py:13
  158.9 173.3 %collective-permute-start.3 = (f32[2,128,256]{2,1,0:T(8,128)S(1)}, f32[2,128,256]{2,1,0:T(8,128)S(1)}, u32[]{:S(2)}, u32[]{:S(2)}) collective-permute-start(f32[2,128,256]{2,1,0:T(8,128)S(1)} %slice.257), channel_id=1, source_target_pairs={{0,32},{32,64},{64,96},{96,128},{128,160},{160,192},{192,224},{1,3... | collective-permute-start | bytes 786440 | tf_op jit(solution)/shard_map/ppermute | solution.py:13
  332.2 1.5 slice.255
  333.7 1.8 collective-permute-done.3
  337.5 654.0 %all-reduce.5.cloned.1.call-done = f32[2,128,128]{2,1,0:T(8,128)} async-done(((f32[2,128,128]{2,1,0:T(8,128)}), f32[2,128,128]{2,1,0:T(8,128)}) %all-reduce.5.cloned.1.call-update) | async-done | bytes 131088 | tf_op jit(solution)/shard_map/psum | solution.py:122
  991.4 1.6 broadcast_divide_fusion
  993.0 32.0 %all-reduce.3.cloned.1.call-done = f32[2,1024,256]{2,1,0:T(8,128)} async-done(((f32[2,1024,256]{2,1,0:T(8,128)}), f32[2,1024,256]{2,1,0:T(8,128)}) %all-reduce.3.cloned.1.call-update) | async-done | bytes 2097168 | tf_op jit(solution)/shard_map/psum | solution.py:121
  1025.0 3.0 copy.42
  (69 shorter events, 32.9 us)
Async XLA Ops:
  7.2 2.8 copy-start.2
  7.2 984.3 %all-reduce.5.cloned.1.call-start = ((), (), s32[]{:S(2)}) async-start(), calls=%async_computation.1 | async-start | bytes 262144 | tf_op jit(solution)/shard_map/psum | solution.py:122
  8.7 28.4 %copy-start.5 = (s32[8,16]{1,0:T(8,128)S(1)}, s32[8,16]{1,0:T(8,128)}, u32[]{:S(2)}) copy-start(s32[8,16]{1,0:T(8,128)} %param.17) | copy-start | bytes 1540
  8.7 25.3 %collective-permute-start = (f32[2,1024,128]{2,1,0:T(8,128)S(1)}, f32[2,1024,128]{2,1,0:T(8,128)S(1)}, u32[]{:S(2)}, u32[]{:S(2)}) collective-permute-start(f32[2,1024,128]{2,1,0:T(8,128)S(1)} %slice.220), channel_id=1, source_target_pairs={{2,0},{4,2},{6,4},{8,6},{10,8},{12,10},{14,12},{16,14},{18,16},{20... | collective-permute-start | bytes 3145736 | tf_op jit(solution)/shard_map/ppermute | solution.py:13
  34.1 1.7 copy-start
  35.8 18.1 %collective-permute-start.1 = (f32[2,128,384]{2,1,0:T(8,128)S(1)}, f32[2,128,384]{2,1,0:T(8,128)S(1)}, u32[]{:S(2)}, u32[]{:S(2)}) collective-permute-start(f32[2,128,384]{2,1,0:T(8,128)S(1)} %slice.254), channel_id=1, source_target_pairs={{32,0},{64,32},{96,64},{128,96},{160,128},{192,160},{224,192},{33,... | collective-permute-start | bytes 1179656 | tf_op jit(solution)/shard_map/ppermute | solution.py:13
  57.8 2.1 copy-start.6
  57.8 2.1 copy-start.7
  59.9 43.6 %copy-start.3 = (bf16[256,256]{1,0:T(8,128)(2,1)}, bf16[256,256]{1,0:T(8,128)(2,1)S(1)}, u32[]{:S(2)}) copy-start(bf16[256,256]{1,0:T(8,128)(2,1)S(1)} %get-tuple-element.384) | copy-start | bytes 393220 | tf_op jit(solution)/shard_map/while
  114.1 27.5 %copy-start.4 = (bf16[256,256]{1,0:T(8,128)(2,1)S(1)}, bf16[256,256]{1,0:T(8,128)(2,1)}, u32[]{:S(2)}) copy-start(bf16[256,256]{1,0:T(8,128)(2,1)} %copy-done.3) | copy-start | bytes 393220 | tf_op jit(solution)/shard_map/while
  141.6 4.6 copy-start.1
  143.0 14.4 %collective-permute-start.2 = (f32[2,1152,128]{2,1,0:T(8,128)S(1)}, f32[2,1152,128]{2,1,0:T(8,128)S(1)}, u32[]{:S(2)}, u32[]{:S(2)}) collective-permute-start(f32[2,1152,128]{2,1,0:T(8,128)S(1)} %slice.224), channel_id=1, source_target_pairs={{0,2},{2,4},{4,6},{6,8},{8,10},{10,12},{12,14},{14,16},{16,18},{18... | collective-permute-start | bytes 3538952 | tf_op jit(solution)/shard_map/ppermute | solution.py:13
  158.9 176.6 %collective-permute-start.3 = (f32[2,128,256]{2,1,0:T(8,128)S(1)}, f32[2,128,256]{2,1,0:T(8,128)S(1)}, u32[]{:S(2)}, u32[]{:S(2)}) collective-permute-start(f32[2,128,256]{2,1,0:T(8,128)S(1)} %slice.257), channel_id=1, source_target_pairs={{0,32},{32,64},{64,96},{96,128},{128,160},{160,192},{192,224},{1,3... | collective-permute-start | bytes 786440 | tf_op jit(solution)/shard_map/ppermute | solution.py:13
  332.2 692.8 %all-reduce.3.cloned.1.call-start = ((), (), s32[]{:S(2)}) async-start(), calls=%async_computation | async-start | bytes 4194304 | tf_op jit(solution)/shard_map/psum | solution.py:121
Sparse Core Ops, SparseCore 0:
  332.3 659.1 all-reduce.4
  994.6 30.3 all-reduce.2
where the time goes:
time: 1050 us; the launch traced here: 1030 us
  waiting for transfers between devices  734 us (70%)
  starting transfers between devices  177 us (17%)
  local copies, waits for them, and re-layouts  57.8 us (6%)
  loops' own time  30.4 us (3%)
  other arithmetic  18 us (2%)
  between operations  15.5 us (1%)
    psum x1, waiting for transfers between devices, shards(): probe_total = lax.psum(probe_acc, ('ty', 'tx', 'pa'))  654 us
    ppermute x4, starting transfers between devices, from_behind(): lax.ppermute(value, axis, [(source, source + steps) for source in range(i...  177 us
    ppermute x4, waiting for transfers between devices, from_behind(): lax.ppermute(value, axis, [(source, source + steps) for source in range(i...  48.5 us
    psum x1, waiting for transfers between devices, shards(): object_grad = lax.psum(tile_grad, 'pa')  32 us
    another operation x1, loops' own time, shards(): grad_field, probe_acc = lax.fori_loop(0, nblocks, block_step, init)  30.4 us
    dynamic_update_slice x8, local copies, waits for them, and re-layouts, block_step(): grad_field = lax.dynamic_update_slice(grad_field, added, where_at)  29.6 us
  transfers between devices with their start and end apart: 6, of which 6 were waited for; matrix products, arithmetic and copies ran while one was open for 1% of the time, Pallas kernels for 0%

commit v1 on v0

--- a/solution.py
+++ b/solution.py
@@ -118,7 +118,7 @@
     lower_strip = grad_field[:, tile_height:, :]
     arrived_below = from_behind(lower_strip, "ty", 1)
     tile_grad = grad_field[:, :tile_height, :].at[:, :width, :].add(arrived_below)
-    object_grad = lax.psum(tile_grad, "pa")
+    object_grad = jnp.sum(lax.all_gather(tile_grad, "pa"), axis=0)
     probe_total = lax.psum(probe_acc, ("ty", "tx", "pa"))
     probe_grad = probe_total / jnp.sum(counts).astype(jnp.float32)
     return (object_grad, probe_grad)

time: 1050 us -> 1000 us (0.952)
  waiting for transfers between devices: 734 us -> 682 us
    psum x1 -> x0, waiting for transfers between devices: 32 us -> none  [shards(): object_grad = lax.psum(tile_grad, 'pa')]
    psum x1, waiting for transfers between devices: 654 us -> 634 us  [shards(): probe_total = lax.psum(probe_acc, ('ty', 'tx', 'pa'))]
  transfers between devices with their start and end apart: 6 -> 6, of which waited for: 6 -> 5; matrix products, arithmetic and copies ran while one was open for 1% -> 1% of each run, Pallas kernels for 0% -> 0%
where the time goes in v1:
time: 1000 us; the launch traced here: 987 us
  waiting for transfers between devices  682 us (68%)
  starting transfers between devices  178 us (18%)
  local copies, waits for them, and re-layouts  55.8 us (6%)
  loops' own time  30.4 us (3%)
  other arithmetic  22.4 us (2%)
  between operations  17 us (2%)
    psum x1, waiting for transfers between devices, shards(): probe_total = lax.psum(probe_acc, ('ty', 'tx', 'pa'))  634 us
    ppermute x4, starting transfers between devices, from_behind(): lax.ppermute(value, axis, [(source, source + steps) for source in range(i...  178 us
    ppermute x4, waiting for transfers between devices, from_behind(): lax.ppermute(value, axis, [(source, source + steps) for source in range(i...  47.9 us
    another operation x1, loops' own time, shards(): grad_field, probe_acc = lax.fori_loop(0, nblocks, block_step, init)  30.4 us
    dynamic_update_slice x8, local copies, waits for them, and re-layouts, block_step(): grad_field = lax.dynamic_update_slice(grad_field, added, where_at)  29.6 us
  transfers between devices with their start and end apart: 6, of which 5 were waited for; matrix products, arithmetic and copies ran while one was open for 1% of the time, Pallas kernels for 0%

profile of v1, /device:TPU:1, one launch (start us, length us, event | category | flops | bytes accessed | tf_op | source)
XLA Modules:
  0.0 987.0 jit_solution(9865679673370901483)
XLA Ops:
  11.0 23.9 %collective-permute-done = f32[2,1024,128]{2,1,0:T(8,128)S(1)} collective-permute-done((f32[2,1024,128]{2,1,0:T(8,128)S(1)}, f32[2,1024,128]{2,1,0:T(8,128)S(1)}, u32[]{:S(2)}, u32[]{:S(2)}) %collective-permute-start) | collective-permute-done | bytes 1048608 | tf_op jit(solution)/shard_map/ppermute | solution.py:13
  34.9 1.7 copy-done
  39.2 3.2 copy.13
  43.0 11.7 %collective-permute-done.1 = f32[2,128,384]{2,1,0:T(8,128)S(1)} collective-permute-done((f32[2,128,384]{2,1,0:T(8,128)S(1)}, f32[2,128,384]{2,1,0:T(8,128)S(1)}, u32[]{:S(2)}, u32[]{:S(2)}) %collective-permute-start.1) | collective-permute-done | bytes 393248 | tf_op jit(solution)/shard_map/ppermute | solution.py:13
  54.7 3.9 pad_maximum_fusion
  58.6 2.0 broadcast_in_dim.23
  60.7 81.8 %while.14 = (s32[]{:T(128)}, f32[2,1152,384]{2,1,0:T(8,128)}, f32[2,128,128]{2,1,0:T(8,128)S(1)}, s32[]{:T(128)}, s32[64]{0:T(128)S(1)}, /*index=5*/s32[64]{0:T(...) while((s32[]{:T(128)}, f32[2,1152,384]{2,1,0:T(8,128)}, ...), condition=%wide.region_3.4_spmd, body=%wide.region_0.3_spmd.sunk | while | flops 546603072 | bytes 25953520 | solution.py:114
  105.4 3.7 dynamic_update_slice.32
  110.2 3.7 dynamic_update_slice.33
  114.9 3.7 dynamic_update_slice.34
  119.8 3.7 dynamic_update_slice.35
  124.6 3.7 dynamic_update_slice.36
  129.3 3.7 dynamic_update_slice.37
  134.1 3.7 dynamic_update_slice.38
  138.8 3.7 dynamic_update_slice.39
  142.5 2.4 slice.224
  144.9 2.3 collective-permute-start.2
  147.2 1.8 slice.222
  149.1 10.5 %collective-permute-done.2 = f32[2,1152,128]{2,1,0:T(8,128)} collective-permute-done((f32[2,1152,128]{2,1,0:T(8,128)}, f32[2,1152,128]{2,1,0:T(8,128)}, u32[]{:S(2)}, u32[]{:S(2)}) %collective-permute-start.2) | collective-permute-done | bytes 1179680 | tf_op jit(solution)/shard_map/ppermute | solution.py:13
  159.6 1.8 add_dynamic-update-slice_fusion
  161.4 173.3 %collective-permute-start.3 = (f32[2,128,256]{2,1,0:T(8,128)S(1)}, f32[2,128,256]{2,1,0:T(8,128)S(1)}, u32[]{:S(2)}, u32[]{:S(2)}) collective-permute-start(f32[2,128,256]{2,1,0:T(8,128)S(1)} %slice.257), channel_id=1, source_target_pairs={{0,32},{32,64},{64,96},{96,128},{128,160},{160,192},{192,224},{1,3... | collective-permute-start | bytes 786440 | tf_op jit(solution)/shard_map/ppermute | solution.py:13
  336.1 1.8 collective-permute-done.3
  340.0 633.9 %all-reduce.2.cloned.1.call-done = f32[2,128,128]{2,1,0:T(8,128)} async-done(((f32[2,128,128]{2,1,0:T(8,128)}), f32[2,128,128]{2,1,0:T(8,128)}) %all-reduce.2.cloned.1.call-update) | async-done | bytes 131088 | tf_op jit(solution)/shard_map/psum | solution.py:122
  975.5 4.0 reduce_sum.36
  (69 shorter events, 31.8 us)
Async XLA Ops:
  8.0 2.8 copy-start.2
  8.0 965.9 %all-reduce.2.cloned.1.call-start = ((), (), s32[]{:S(2)}) async-start(), calls=%async_computation.1 | async-start | bytes 262144 | tf_op jit(solution)/shard_map/psum | solution.py:122
  9.5 28.4 %copy-start.5 = (s32[8,16]{1,0:T(8,128)S(1)}, s32[8,16]{1,0:T(8,128)}, u32[]{:S(2)}) copy-start(s32[8,16]{1,0:T(8,128)} %param.17) | copy-start | bytes 1540
  9.5 25.3 %collective-permute-start = (f32[2,1024,128]{2,1,0:T(8,128)S(1)}, f32[2,1024,128]{2,1,0:T(8,128)S(1)}, u32[]{:S(2)}, u32[]{:S(2)}) collective-permute-start(f32[2,1024,128]{2,1,0:T(8,128)S(1)} %slice.220), channel_id=1, source_target_pairs={{2,0},{4,2},{6,4},{8,6},{10,8},{12,10},{14,12},{16,14},{18,16},{20... | collective-permute-start | bytes 3145736 | tf_op jit(solution)/shard_map/ppermute | solution.py:13
  34.9 1.7 copy-start
  36.6 18.1 %collective-permute-start.1 = (f32[2,128,384]{2,1,0:T(8,128)S(1)}, f32[2,128,384]{2,1,0:T(8,128)S(1)}, u32[]{:S(2)}, u32[]{:S(2)}) collective-permute-start(f32[2,128,384]{2,1,0:T(8,128)S(1)} %slice.254), channel_id=1, source_target_pairs={{32,0},{64,32},{96,64},{128,96},{160,128},{192,160},{224,192},{33,... | collective-permute-start | bytes 1179656 | tf_op jit(solution)/shard_map/ppermute | solution.py:13
  58.6 2.1 copy-start.6
  58.6 2.1 copy-start.7
  60.7 43.6 %copy-start.3 = (bf16[256,256]{1,0:T(8,128)(2,1)}, bf16[256,256]{1,0:T(8,128)(2,1)S(1)}, u32[]{:S(2)}) copy-start(bf16[256,256]{1,0:T(8,128)(2,1)S(1)} %get-tuple-element.384) | copy-start | bytes 393220 | tf_op jit(solution)/shard_map/while
  114.9 27.5 %copy-start.4 = (bf16[256,256]{1,0:T(8,128)(2,1)S(1)}, bf16[256,256]{1,0:T(8,128)(2,1)}, u32[]{:S(2)}) copy-start(bf16[256,256]{1,0:T(8,128)(2,1)} %copy-done.3) | copy-start | bytes 393220 | tf_op jit(solution)/shard_map/while
  142.4 6.6 copy-start.1
  144.9 14.7 %collective-permute-start.2 = (f32[2,1152,128]{2,1,0:T(8,128)}, f32[2,1152,128]{2,1,0:T(8,128)}, u32[]{:S(2)}, u32[]{:S(2)}) collective-permute-start(f32[2,1152,128]{2,1,0:T(8,128)} %slice.224), channel_id=1, source_target_pairs={{0,2},{2,4},{4,6},{6,8},{8,10},{10,12},{12,14},{14,16},{16,18},{18... | collective-permute-start | bytes 3538952 | tf_op jit(solution)/shard_map/ppermute | solution.py:13
  149.0 826.4 %all-gather.2.cloned.1.call-start = ((), (), s32[]{:S(2)}) async-start(), calls=%async_computation | async-start | bytes 6291456 | tf_op jit(solution)/shard_map/all_gather | solution.py:121
  161.4 176.6 %collective-permute-start.3 = (f32[2,128,256]{2,1,0:T(8,128)S(1)}, f32[2,128,256]{2,1,0:T(8,128)S(1)}, u32[]{:S(2)}, u32[]{:S(2)}) collective-permute-start(f32[2,128,256]{2,1,0:T(8,128)S(1)} %slice.257), channel_id=1, source_target_pairs={{0,32},{32,64},{64,96},{96,128},{128,160},{160,192},{192,224},{1,3... | collective-permute-start | bytes 786440 | tf_op jit(solution)/shard_map/ppermute | solution.py:13
Sparse Core Ops, SparseCore 0:
  149.2 824.6 all-reduce.1
Sparse Core Ops, SparseCore 1:
  338.8 444.2 all-gather.1
